TPU v7x, 32 devices: a whole 2x2x4 slice. The times are simulated.
32 devices in a mesh: shard: 4 (over y, core), ctx: 4 (over z), tp: 2 (over x).
Axes of the slice: x: 2, y: 2, z: 4, core: 2. Of those that a mesh axis runs over, the one named last changes fastest.
Arguments:
- tokens: bfloat16 [8, 1024, 768], P('shard', 'ctx'), may hold values from -4 to 4
- lengths: int32 [8], P('shard'), may hold values from 256 to 1024, as said below
- w_qkv: float32 [768, 3, 768], P(('shard', 'ctx'), None, 'tp'), may hold values from -0.21875 to 0.21875
- b_qv: float32 [2, 768], P(None, 'tp'), may hold values from -3 to 3
- w_out: float32 [768, 768], P('tp', ('shard', 'ctx')), may hold values from -0.625 to 0.625
- w_gu: float32 [768, 2, 3072], P(('shard', 'ctx'), None, 'tp'), may hold values from -0.21875 to 0.21875
- w_down: float32 [3072, 768], P('tp', ('shard', 'ctx')), may hold values from -0.109375 to 0.109375
- vectors: float32 [6, 768], replicated, may hold values from 0.25 to 1.75
- cotangent: bfloat16 [8, 1024, 768], P('shard', 'ctx'), may hold values from -6 to 6
Outputs:
- output: bfloat16 [8, 1024, 768], P('shard', 'ctx')
- input_grad: float32 [8, 1024, 768], P('shard', 'ctx')
- grad_qkv: float32 [768, 3, 768], P(('shard', 'ctx'), None, 'tp')
- grad_bqv: float32 [2, 768], P(None, 'tp')
- grad_out: float32 [768, 768], P('tp', ('shard', 'ctx'))
- grad_gu: float32 [768, 2, 3072], P(('shard', 'ctx'), None, 'tp')
- grad_down: float32 [3072, 768], P('tp', ('shard', 'ctx'))
- grad_vectors: float32 [6, 768], replicated
Inputs may be any that keep to these rules, and one draw needn't show every extreme that they name: `lengths`: sequence 0 has all 1024 slots valid and sequence 1 has 256.
All inputs are finite; a program needn't handle non-finite values.
Results may differ from a plain program's by a relative error of at most 0.018.
Values may be sent and summed in bfloat16 or wider, within the bound.
No kernel may reach another device: no remote copies, remote signals or barrier semaphores. Data moves between devices by JAX's collectives and lax.ppermute only.
A program may use at most 128 MiB of HBM per device.

v0:
```python
import math
import jax
import jax.numpy as jnp
from jax import lax
from jax.sharding import PartitionSpec as P

H = 12
HD = 64
epsilon = 1e-12


def alibi_slopes(first_head, head_count):
    power = 2 ** (H.bit_length() - 1)
    heads_index = first_head + jnp.arange(head_count, dtype=jnp.int32)
    early = -8.0 * (heads_index + 1).astype(jnp.float32) / power
    later = -4.0 * (2 * (heads_index - power) + 1).astype(jnp.float32) / power
    return jnp.exp2(jnp.where(heads_index < power, early, later))


def layer_norm(values, gain, shift):
    centred = values - jnp.mean(values, axis=-1, keepdims=True)
    spread = jnp.mean(centred * centred, axis=-1, keepdims=True)
    return centred * lax.rsqrt(spread + epsilon) * gain + shift


def gated_unit(gate_input, upper):
    return jax.nn.gelu(gate_input, approximate=False) * upper


def score_block(query_heads, key_heads, query_place, key_place, slopes, lengths):
    scores = (
        jnp.einsum("sqhe,skhe->shqk", query_heads, key_heads, preferred_element_type=jnp.float32)
        * 0.125
    )
    distance = jnp.abs(query_place[:, None] - key_place[None, :]).astype(jnp.float32)
    scores = scores - slopes[None, :, None, None] * distance[None, None]
    usable = key_place[None, :] < lengths[:, None]
    return jnp.where(usable[:, None, None, :], jnp.exp(scores), 0.0)


def backward_scores(
    query_heads,
    numer_heads,
    correction,
    key_heads,
    value_heads,
    query_place,
    key_place,
    slopes,
    lengths,
):
    weights = score_block(query_heads, key_heads, query_place, key_place, slopes, lengths)
    value_dots = jnp.einsum(
        "sqhe,skhe->shqk", numer_heads, value_heads, preferred_element_type=jnp.float32
    )
    grad_scores = (weights * (value_dots - correction[..., None])).astype(jnp.bfloat16)
    return (weights.astype(jnp.bfloat16), grad_scores)


def split_blocks(shard_piece, slot_count, ctx_count):
    piece_rows = shard_piece.shape[1]
    block_rows = math.gcd(piece_rows, 128)
    block_count = piece_rows // block_rows
    shaped = shard_piece.reshape(
        (shard_piece.shape[0], block_count, block_rows) + shard_piece.shape[2:]
    )
    blocks = jnp.moveaxis(shaped, 1, 0)
    row_ids = jnp.arange(piece_rows, dtype=jnp.int32)
    places = (row_ids % slot_count * ctx_count + row_ids // slot_count).reshape(
        block_count, block_rows
    )
    offsets = block_rows * jnp.arange(block_count, dtype=jnp.int32)
    return (blocks, places, offsets)


def on_device(tokens, lengths, w_qkv, b_qv, w_out, w_gu, w_down, vectors, cotangent):
    ctx_count = lax.axis_size("ctx")
    ctx_rank = lax.axis_index("ctx")
    seq_count, slot_count, model_width = tokens.shape
    local_width = b_qv.shape[1]
    head_count = local_width // HD
    slopes = alibi_slopes(lax.axis_index("tp") * head_count, head_count)
    slot_ids = jnp.arange(slot_count, dtype=jnp.int32)
    query_place = slot_ids * ctx_count + ctx_rank
    query_live = (query_place[None, :] < lengths[:, None]).astype(jnp.float32)
    live_rows = query_live[:, :, None]
    head_shape = (seq_count, slot_count, head_count, HD)
    whole_qkv, whole_out, whole_gu, whole_down = (
        lax.all_gather(w_qkv.astype(jnp.bfloat16), ("shard", "ctx"), axis=0, tiled=True),
        lax.all_gather(w_out.astype(jnp.bfloat16), ("shard", "ctx"), axis=1, tiled=True),
        lax.all_gather(w_gu.astype(jnp.bfloat16), ("shard", "ctx"), axis=0, tiled=True),
        lax.all_gather(w_down.astype(jnp.bfloat16), ("shard", "ctx"), axis=1, tiled=True),
    )
    inputs = tokens.astype(jnp.float32)
    projected = jnp.einsum("std,dcm->stcm", tokens, whole_qkv, preferred_element_type=jnp.float32)
    query_rows = (projected[:, :, 0] + b_qv[0]).astype(jnp.bfloat16)
    key_rows = projected[:, :, 1].astype(jnp.bfloat16)
    value_rows = (projected[:, :, 2] + b_qv[1]).astype(jnp.bfloat16)
    query_heads = query_rows.reshape(head_shape)
    pairs = jnp.stack([key_rows, value_rows], axis=2)
    start_numer = jnp.zeros((seq_count, head_count, slot_count, HD), jnp.float32)
    start_denom = jnp.zeros((seq_count, head_count, slot_count), jnp.float32)
    blocks, places, offsets = split_blocks(
        lax.all_gather(pairs, "ctx", axis=1, tiled=True), slot_count, ctx_count
    )

    def forward_advance(inner_state, block_item):
        key_block, key_place, row_offset = block_item
        numerator, denominator = inner_state
        key_heads = key_block[:, :, 0].reshape(seq_count, -1, head_count, HD)
        value_heads = key_block[:, :, 1].reshape(seq_count, -1, head_count, HD)
        weights = score_block(query_heads, key_heads, query_place, key_place, slopes, lengths)
        numerator = numerator + jnp.einsum(
            "shqk,skhe->shqe",
            weights.astype(jnp.bfloat16),
            value_heads,
            preferred_element_type=jnp.float32,
        )
        return ((numerator, denominator + jnp.sum(weights, axis=-1)), None)

    result_state, unused = lax.scan(
        forward_advance, (start_numer, start_denom), (blocks, places, offsets)
    )
    numerator, denominator = result_state
    denominator = denominator + (1.0 - query_live)[:, None, :]
    attention_q = jnp.transpose(numerator / denominator[..., None], (0, 2, 1, 3))
    denom_q = jnp.transpose(denominator, (0, 2, 1))
    mixed = attention_q.reshape(seq_count, slot_count, local_width).astype(jnp.bfloat16)
    attn_part = jnp.einsum("stm,mn->stn", mixed, whole_out, preferred_element_type=jnp.float32)
    attn_branch = lax.psum(attn_part, "tp") + vectors[4]
    hidden, first_pull = jax.vjp(layer_norm, inputs + attn_branch, vectors[0], vectors[1])
    hidden_low = hidden.astype(jnp.bfloat16)
    gated = jnp.einsum("std,dcf->stcf", hidden_low, whole_gu, preferred_element_type=jnp.float32)
    activated, unit_pull = jax.vjp(gated_unit, gated[:, :, 0], gated[:, :, 1])
    act_low = activated.astype(jnp.bfloat16)
    ffn_part = jnp.einsum("stf,fn->stn", act_low, whole_down, preferred_element_type=jnp.float32)
    ffn_branch = lax.psum(ffn_part, "tp") + vectors[5]
    normed, second_pull = jax.vjp(layer_norm, hidden + ffn_branch, vectors[2], vectors[3])
    output = (normed * live_rows).astype(jnp.bfloat16)
    upstream = cotangent.astype(jnp.float32) * live_rows
    grad_second, grad_gain_two, grad_shift_two = second_pull(upstream)
    grad_ffn = grad_second.astype(jnp.bfloat16)
    grad_down = jnp.einsum("stf,stn->fn", act_low, grad_ffn, preferred_element_type=jnp.float32)
    grad_ffn_bias = jnp.sum(grad_ffn.astype(jnp.float32), axis=(0, 1))
    grad_act = jnp.einsum("stn,fn->stf", grad_ffn, whole_down, preferred_element_type=jnp.float32)
    grad_gate, grad_upper = unit_pull(grad_act)
    grad_gated = jnp.stack([grad_gate, grad_upper], axis=2).astype(jnp.bfloat16)
    grad_gu = jnp.einsum(
        "std,stcf->dcf", hidden_low, grad_gated, preferred_element_type=jnp.float32
    )
    hidden_part = jnp.einsum(
        "stcf,dcf->std", grad_gated, whole_gu, preferred_element_type=jnp.float32
    )
    grad_hidden = grad_second + lax.psum(hidden_part, "tp")
    grad_first, grad_gain_one, grad_shift_one = first_pull(grad_hidden)
    grad_attn = grad_first.astype(jnp.bfloat16)
    grad_out = jnp.einsum("stm,stn->mn", mixed, grad_attn, preferred_element_type=jnp.float32)
    grad_out_bias = jnp.sum(grad_attn.astype(jnp.float32), axis=(0, 1))
    grad_mixed = jnp.einsum(
        "stn,mn->stm", grad_attn, whole_out, preferred_element_type=jnp.float32
    ).astype(jnp.bfloat16)
    grad_mixed_heads = grad_mixed.reshape(head_shape).astype(jnp.float32)
    correction = jnp.transpose(
        jnp.sum(grad_mixed_heads * attention_q, axis=-1) / denom_q, (0, 2, 1)
    )
    numer_heads = (grad_mixed_heads / denom_q[..., None]).astype(jnp.bfloat16)
    start_query = jnp.zeros(head_shape, jnp.float32)
    start_state = (
        start_query,
        jnp.zeros((seq_count, slot_count * ctx_count, 2, local_width), jnp.float32),
    )
    blocks, places, offsets = split_blocks(
        lax.all_gather(pairs, "ctx", axis=1, tiled=True), slot_count, ctx_count
    )

    def backward_advance(current_state, block_item):
        key_block, key_place, row_offset = block_item
        key_heads = key_block[:, :, 0].reshape(seq_count, -1, head_count, HD)
        value_heads = key_block[:, :, 1].reshape(seq_count, -1, head_count, HD)
        weights_low, grad_scores = backward_scores(
            query_heads,
            numer_heads,
            correction,
            key_heads,
            value_heads,
            query_place,
            key_place,
            slopes,
            lengths,
        )
        grad_query = current_state[0] + jnp.einsum(
            "shqk,skhe->sqhe", grad_scores, key_heads, preferred_element_type=jnp.float32
        )
        grad_key = (
            jnp.einsum(
                "shqk,sqhe->skhe", grad_scores, query_heads, preferred_element_type=jnp.float32
            )
            * 0.125
        )
        grad_value = jnp.einsum(
            "shqk,sqhe->skhe", weights_low, numer_heads, preferred_element_type=jnp.float32
        )
        stacked = jnp.stack(
            [
                grad_key.reshape(seq_count, -1, local_width),
                grad_value.reshape(seq_count, -1, local_width),
            ],
            axis=2,
        )
        buffer = lax.dynamic_update_slice_in_dim(current_state[1], stacked, row_offset, axis=1)
        return ((grad_query, buffer), None)

    result_state, unused = lax.scan(backward_advance, start_state, (blocks, places, offsets))
    grad_pairs = lax.psum_scatter(
        result_state[1].astype(jnp.bfloat16), "ctx", scatter_dimension=1, tiled=True
    )
    grad_query_low = (
        (result_state[0] * 0.125).astype(jnp.bfloat16).reshape(seq_count, slot_count, local_width)
    )
    grad_proj = jnp.concatenate([grad_query_low[:, :, None], grad_pairs], axis=2)
    grad_qkv = jnp.einsum("std,stcm->dcm", tokens, grad_proj, preferred_element_type=jnp.float32)
    bias_terms = jnp.stack(
        [
            jnp.sum(grad_query_low.astype(jnp.float32), axis=(0, 1)),
            jnp.sum(grad_pairs[:, :, 1].astype(jnp.float32), axis=(0, 1)),
        ]
    )
    input_part = jnp.einsum(
        "stcm,dcm->std", grad_proj, whole_qkv, preferred_element_type=jnp.float32
    )
    input_grad = grad_first + lax.psum(input_part.astype(jnp.bfloat16), "tp").astype(jnp.float32)
    grad_weights = (
        lax.psum_scatter(grad_qkv, ("shard", "ctx"), scatter_dimension=0, tiled=True),
        lax.psum_scatter(grad_out, ("shard", "ctx"), scatter_dimension=1, tiled=True),
        lax.psum_scatter(grad_gu, ("shard", "ctx"), scatter_dimension=0, tiled=True),
        lax.psum_scatter(grad_down, ("shard", "ctx"), scatter_dimension=1, tiled=True),
    )
    vector_terms = jnp.stack(
        [grad_gain_one, grad_shift_one, grad_gain_two, grad_shift_two, grad_out_bias, grad_ffn_bias]
    )
    grad_bqv, grad_vectors = lax.psum((bias_terms, vector_terms), ("shard", "ctx"))
    return (
        output,
        input_grad,
        grad_weights[0],
        grad_bqv,
        grad_weights[1],
        grad_weights[2],
        grad_weights[3],
        grad_vectors,
    )


def solution(mesh):
    placed = (
        P("shard", "ctx", None),
        P("shard"),
        P(("shard", "ctx"), None, "tp"),
        P(None, "tp"),
        P("tp", ("shard", "ctx")),
        P(("shard", "ctx"), None, "tp"),
        P("tp", ("shard", "ctx")),
        P(),
        P("shard", "ctx", None),
    )
    return jax.shard_map(
        on_device,
        mesh=mesh,
        in_specs=placed,
        out_specs=(
            P("shard", "ctx", None),
            P("shard", "ctx", None),
            P(("shard", "ctx"), None, "tp"),
            P(None, "tp"),
            P("tp", ("shard", "ctx")),
            P(("shard", "ctx"), None, "tp"),
            P("tp", ("shard", "ctx")),
            P(),
        ),
        check_vma=False,
    )
```

profile of v0, /device:TPU:0, one launch (start us, length us, event | category | flops | bytes accessed | tf_op | source)
XLA Modules:
  0.0 1021.4 jit_solution(10620313028883199364)
XLA Ops:
  9.7 44.3 %all-gather.5.cloned.1.call-done = bf16[768,3,384]{2,0,1:T(8,128)(2,1)} async-done(((bf16[48,3,384]{2,0,1:T(8,128)(2,1)}), bf16[768,3,384]{2,0,1:T(8,128)(2,1)}) %all-gather.5.cloned.1.call-update) | async-done | bytes 1769488 | tf_op jit(solution)/shard_map/all_gather | solution.py:89
  60.1 47.1 %all_gather.18 = bf16[384,768]{0,1:T(8,128)(2,1)S(1)} all-gather(bf16[384,48]{0,1:T(8,128)(2,1)S(1)} %convert_element_type.137), channel_id=1, replica_groups=mesh['shard'=4,'ctx'=4,'tp'=2] {'shard','ctx'}, dimensions={1}, use_global_device_ids=true | all-gather | bytes 626688 | tf_op jit(solution)/shard_map/all_gather | solution.py:90
  107.6 22.3 %all-gather.7.cloned.1.call-done = bf16[2,1024,2,384]{3,1,2,0:T(8,128)(2,1)} async-done(((bf16[2,256,2,384]{3,1,2,0:T(8,128)(2,1)}), bf16[2,1024,2,384]{3,1,2,0:T(8,128)(2,1)}) %all-gather.7.cloned.1.call-update) | async-done | bytes 3145744 | tf_op jit(solution)/shard_map/all_gather | solution.py:104
  129.9 4.7 copy.62
  134.6 29.5 %while.26 = (s32[]{:T(128)}, f32[2,6,256,64]{2,3,1,0:T(8,128)S(1)}, f32[2,6,256]{2,1,0:T(8,128)S(1)}, s32[8,128]{1,0:T(8,128)}, s32[2]{0:T(128)}, /*index=5*/bf1...) while((s32[]{:T(128)}, f32[2,6,256,64]{2,3,1,0:T(8,128)S(1)}, ...), condition=%wide.region_2.3_spmd.clone, body=%wide.region_0.2_spmd.clone.sunk | while | flops 103321416 | bytes 7393984 | solution.py:121
  168.9 48.1 %all-reduce.8.cloned.1.call-done = f32[2,256,768]{2,1,0:T(8,128)} async-done(((f32[2,256,768]{2,1,0:T(8,128)}), f32[2,256,768]{2,1,0:T(8,128)}) %all-reduce.8.cloned.1.call-update) | async-done | bytes 1572880 | tf_op jit(solution)/shard_map/psum | solution.py:130
  219.0 53.9 %all-gather.9.cloned.1.call-done = bf16[768,2,1536]{2,0,1:T(8,128)(2,1)} async-done(((bf16[48,2,1536]{2,0,1:T(8,128)(2,1)}), bf16[768,2,1536]{2,0,1:T(8,128)(2,1)}) %all-gather.9.cloned.1.call-update) | async-done | bytes 4718608 | tf_op jit(solution)/shard_map/all_gather | solution.py:91
  273.0 4.7 fusion.23
  280.3 7.7 multiply_convert_fusion.1
  288.0 28.5 %all-gather.11.cloned.1.call-done = bf16[1536,768]{0,1:T(8,128)(2,1)} async-done(((bf16[1536,48]{0,1:T(8,128)(2,1)}), bf16[1536,768]{0,1:T(8,128)(2,1)}) %all-gather.11.cloned.1.call-update) | async-done | bytes 2359312 | tf_op jit(solution)/shard_map/all_gather | solution.py:92
  316.6 4.2 fusion.48
  322.8 48.5 %all-reduce.10.cloned.1.call-done = f32[2,256,768]{2,1,0:T(8,128)} async-done(((f32[2,256,768]{2,1,0:T(8,128)}), f32[2,256,768]{2,1,0:T(8,128)}) %all-reduce.10.cloned.1.call-update) | async-done | bytes 1572880 | tf_op jit(solution)/shard_map/psum | solution.py:137
  383.5 3.8 fusion.60
  389.2 49.7 %all-reduce.12.cloned.1.call-done = f32[2,256,768]{2,1,0:T(8,128)} async-done(((f32[2,256,768]{2,1,0:T(8,128)}), f32[2,256,768]{2,1,0:T(8,128)}) %all-reduce.12.cloned.1.call-update) | async-done | bytes 1572880 | tf_op jit(solution)/shard_map/psum | solution.py:154
  439.0 4.4 multiply_reduce_fusion.1
  449.4 88.8 %while.27 = (s32[]{:T(128)}, f32[2,256,6,64]{1,3,2,0:T(8,128)S(1)}, bf16[2,1024,2,384]{3,1,2,0:T(8,128)(2,1)}, bf16[8,2,128,2,384]{2,4,1,3,0:T(8,128)(2,1)}, s32...) while((s32[]{:T(128)}, f32[2,256,6,64]{1,3,2,0:T(8,128)S(1)}, ...), condition=%wide.region_16.17_spmd.clone, body=%wide.region_15.16_spmd.clone.sunk | while | flops 255492928 | bytes 16990992 | solution.py:213
  467.8 3.6 dynamic_update_slice.5
  479.0 3.6 dynamic_update_slice.5
  490.2 3.6 dynamic_update_slice.5
  501.3 3.6 dynamic_update_slice.5
  512.5 3.6 dynamic_update_slice.5
  523.7 3.6 dynamic_update_slice.5
  538.8 59.9 %reduce-scatter.5.cloned.1.call-done = bf16[2,256,2,384]{3,1,2,0:T(8,128)(2,1)} async-done(((bf16[2,1024,2,384]{3,1,2,0:T(8,128)(2,1)}), bf16[2,256,2,384]{3,1,2,0:T(8,128)(2,1)}) %reduce-scatter.5.cloned.1.call-update) | async-done | bytes 786448 | tf_op jit(solution)/shard_map/reduce_scatter | solution.py:214
  598.7 3.9 bitcast_convert_fusion
  605.6 6.3 copy.71
  613.8 7.9 convolution_bitcast_fusion.1
  624.7 3.6 convolution_bitcast_fusion.2
  630.6 62.4 %all-reduce.1 = (f32[2,384]{1,0:T(2,128)}, f32[6,768]{1,0:T(8,128)}) all-reduce(f32[2,384]{1,0:T(2,128)S(1)} %pad_maximum_fusion.10, f32[6,768]{1,0:T(8,128)S(1)} %stack.63), channel_id=1, replica_groups=mesh['shard'=4,'ctx'=4,'tp'=2] {'shard','ctx'}, use_global_device_ids=true, to_apply=%region_22.23 | all-reduce | flops 5376 | bytes 43008 | tf_op jit(solution)/shard_map/psum | solution.py:241
  695.6 63.3 %all-reduce.16.cloned.1.call-done = f32[768,3,384]{2,1,0:T(4,128)} async-done(((f32[768,3,384]{2,1,0:T(4,128)}), f32[768,3,384]{2,1,0:T(4,128)}) %all-reduce.16.cloned.1.call-update) | async-done | bytes 3538960
  760.6 113.3 %reduce-scatter.9.cloned.1.call-done = f32[48,2,1536]{2,0,1:T(8,128)} async-done(((f32[768,2,1536]{2,0,1:T(8,128)}), f32[48,2,1536]{2,0,1:T(8,128)}) %reduce-scatter.9.cloned.1.call-update) | async-done | bytes 589840 | tf_op jit(solution)/shard_map/reduce_scatter | solution.py:235
  876.3 59.6 %reduce-scatter.7.cloned.1.call-done = f32[384,48]{0,1:T(8,128)} async-done(((f32[384,768]{0,1:T(8,128)}), f32[384,48]{0,1:T(8,128)}) %reduce-scatter.7.cloned.1.call-update) | async-done | bytes 73744 | tf_op jit(solution)/shard_map/reduce_scatter | solution.py:234
  935.8 79.1 %reduce-scatter.11.cloned.1.call-done = f32[1536,48]{0,1:T(8,128)} async-done(((f32[1536,768]{0,1:T(8,128)}), f32[1536,48]{0,1:T(8,128)}) %reduce-scatter.11.cloned.1.call-update) | async-done | bytes 294928 | tf_op jit(solution)/shard_map/reduce_scatter | solution.py:236
  (457 shorter events, 136.4 us)
Async XLA Ops:
  7.2 46.8 %all-gather.5.cloned.1.call-start = ((), (), s32[]{:S(2)}) async-start(), calls=%async_computation.4 | async-start | bytes 1880064 | tf_op jit(solution)/shard_map/all_gather | solution.py:89
  8.8 121.1 %all-gather.7.cloned.1.call-start = ((), (), s32[]{:S(2)}) async-start(), calls=%async_computation.5 | async-start | bytes 3932160 | tf_op jit(solution)/shard_map/all_gather | solution.py:104
  58.1 158.9 %all-reduce.8.cloned.1.call-start = ((), (), s32[]{:S(2)}) async-start(), calls=%async_computation.6 | async-start | bytes 3145728 | tf_op jit(solution)/shard_map/psum | solution.py:130
  58.2 49.3 %copy-start.60 = (s32[256]{0:T(256)}, s32[256]{0:T(256)S(1)}, u32[]{:S(2)}) copy-start(s32[256]{0:T(256)S(1)} %multiply_add_fusion.6) | copy-start | bytes 3076
  107.2 56.9 %copy-start.11 = (bf16[384,768]{0,1:T(8,128)(2,1)}, bf16[384,768]{0,1:T(8,128)(2,1)S(1)}, u32[]{:S(2)}) copy-start(bf16[384,768]{0,1:T(8,128)(2,1)S(1)} %all_gather.18) | copy-start | bytes 1769476
  134.6 29.5 %copy-start.42 = (f32[2,256]{1,0:T(2,128)S(1)}, f32[2,256]{1,0:T(2,128)}, u32[]{:S(2)}) copy-start(f32[2,256]{1,0:T(2,128)} %broadcast_subtract_fusion) | copy-start | bytes 6148
  166.5 50.5 %copy-start.18 = (bf16[2,256,768]{2,1,0:T(8,128)(2,1)S(1)}, bf16[2,256,768]{2,1,0:T(8,128)(2,1)}, u32[]{:S(2)}) copy-start(bf16[2,256,768]{2,1,0:T(8,128)(2,1)} %param.13) | copy-start | bytes 2359300
  166.6 106.4 %all-gather.9.cloned.1.call-start = ((), (), s32[]{:S(2)}) async-start(), calls=%async_computation.7 | async-start | bytes 5013504 | tf_op jit(solution)/shard_map/all_gather | solution.py:91
  167.5 149.1 %all-gather.11.cloned.1.call-start = ((), (), s32[]{:S(2)}) async-start(), calls=%async_computation.8 | async-start | bytes 2506752 | tf_op jit(solution)/shard_map/all_gather | solution.py:92
  168.2 203.0 %all-reduce.10.cloned.1.call-start = ((), (), s32[]{:S(2)}) async-start(), calls=%async_computation.9 | async-start | bytes 3145728 | tf_op jit(solution)/shard_map/psum | solution.py:137
  168.9 104.0 %copy-start.30 = (f32[768]{0:T(1024)}, f32[768]{0:T(1024)S(1)}, u32[]{:S(2)}) copy-start(f32[768]{0:T(1024)S(1)} %get-tuple-element.239) | copy-start | bytes 9220
  168.9 104.0 %copy-start.57 = (f32[768]{0:T(1024)}, f32[768]{0:T(1024)S(1)}, u32[]{:S(2)}) copy-start(f32[768]{0:T(1024)S(1)} %get-tuple-element.238) | copy-start | bytes 9220
  218.7 224.7 %copy-start = (f32[2,256,768]{2,1,0:T(8,128)}, f32[2,256,768]{2,1,0:T(8,128)S(1)}, u32[]{:S(2)}) copy-start(f32[2,256,768]{2,1,0:T(8,128)S(1)} %get-tuple-element.302) | copy-start | bytes 4718596
  218.7 54.3 %copy-start.34 = (f32[2,256]{1,0:T(2,128)}, f32[2,256]{1,0:T(2,128)S(1)}, u32[]{:S(2)}) copy-start(f32[2,256]{1,0:T(2,128)S(1)} %broadcast_multiply_fusion.3) | copy-start | bytes 6148
  219.0 53.9 %copy-start.48 = (f32[2,256]{1,0:T(2,128)}, f32[2,256]{1,0:T(2,128)S(1)}, u32[]{:S(2)}) copy-start(f32[2,256]{1,0:T(2,128)S(1)} %multiply_reduce_fusion.5) | copy-start | bytes 6148
  219.0 53.9 %copy-start.39 = (f32[2,256]{1,0:T(2,128)}, f32[2,256]{1,0:T(2,128)S(1)}, u32[]{:S(2)}) copy-start(f32[2,256]{1,0:T(2,128)S(1)} %fusion.83) | copy-start | bytes 6148
  288.0 32.8 %copy-start.16 = (bf16[2,256,1536]{2,1,0:T(8,128)(2,1)}, bf16[2,256,1536]{2,1,0:T(8,128)(2,1)S(1)}, u32[]{:S(2)}) copy-start(bf16[2,256,1536]{2,1,0:T(8,128)(2,1)S(1)} %get-tuple-element.299) | copy-start | bytes 4718596
  320.8 118.2 %all-reduce.12.cloned.1.call-start = ((), (), s32[]{:S(2)}) async-start(), calls=%async_computation.10 | async-start | bytes 3145728 | tf_op jit(solution)/shard_map/psum | solution.py:154
  371.2 7.0 slice-start
  373.4 4.9 slice-start.1
  377.0 6.5 slice-start.2
  379.0 4.5 slice-start.3
  387.3 211.4 %reduce-scatter.5.cloned.1.call-start = ((), (), s32[]{:S(2)}) async-start(), calls=%async_computation.11 | async-start | bytes 3932160 | tf_op jit(solution)/shard_map/reduce_scatter | solution.py:214
  439.0 4.4 copy-start.40
  538.2 154.9 %all-reduce.14.cloned.1.call-start = ((), (), s32[]{:S(2)}) async-start(), calls=%async_computation.12 | async-start | bytes 1572864 | tf_op jit(solution)/shard_map/psum | solution.py:231
  538.8 63.9 %copy-start.19 = (bf16[2,256,768]{2,1,0:T(8,128)(2,1)S(1)}, bf16[2,256,768]{2,1,0:T(8,128)(2,1)}, u32[]{:S(2)}) copy-start(bf16[2,256,768]{2,1,0:T(8,128)(2,1)} %param.13) | copy-start | bytes 2359300
  602.7 156.2 %all-reduce.16.cloned.1.call-start = ((), (), s32[]{:S(2)}) async-start(), calls=%async_computation.16 | async-start | bytes 9437184
  612.0 261.9 %reduce-scatter.9.cloned.1.call-start = ((), (), s32[]{:S(2)}) async-start(), calls=%async_computation.14 | async-start | bytes 10027008 | tf_op jit(solution)/shard_map/reduce_scatter | solution.py:235
  621.8 314.0 %reduce-scatter.7.cloned.1.call-start = ((), (), s32[]{:S(2)}) async-start(), calls=%async_computation.13 | async-start | bytes 1253376 | tf_op jit(solution)/shard_map/reduce_scatter | solution.py:234
  624.7 390.2 %reduce-scatter.11.cloned.1.call-start = ((), (), s32[]{:S(2)}) async-start(), calls=%async_computation.15 | async-start | bytes 5013504 | tf_op jit(solution)/shard_map/reduce_scatter | solution.py:236
  628.4 64.6 %copy-start.6 = (f32[2,256,768]{2,1,0:T(8,128)S(1)}, f32[2,256,768]{2,1,0:T(8,128)}, u32[]{:S(2)}) copy-start(f32[2,256,768]{2,1,0:T(8,128)} %copy-done.5) | copy-start | bytes 4718596
  628.4 64.6 %copy-start.47 = (f32[2,256]{1,0:T(2,128)S(1)}, f32[2,256]{1,0:T(2,128)}, u32[]{:S(2)}) copy-start(f32[2,256]{1,0:T(2,128)} %copy-done.46) | copy-start | bytes 6148
  (53 other events, 104.5 us)
Sparse Core Ops, SparseCore 0:
  10.8 43.1 all-gather.4
  58.2 71.6 all-gather.6
  166.7 50.2 all-reduce.7
  219.8 53.1 all-gather.8
  275.7 40.8 all-gather.10
  321.0 50.2 all-reduce.9
  387.4 51.5 all-reduce.11
  538.3 60.3 reduce-scatter.4
  602.8 34.2 all-reduce.13
  640.6 118.2 all-reduce.15
  763.0 110.8 reduce-scatter.8
  878.0 57.8 reduce-scatter.6
  940.2 74.5 reduce-scatter.10
where the time goes:
time: 1020 us
  waiting for transfers between devices  671 us (66%)
  blocking collectives  109 us (11%)
  local copies, waits for them, and re-layouts  94.3 us (9%)
  matrix products  63.8 us (6%)
  other arithmetic  49.9 us (5%)
  loops' own time  16.9 us (2%)
  between operations  15.4 us (2%)
    reduce_scatter x1, waiting for transfers between devices, on_device(): lax.psum_scatter(grad_gu, ('shard', 'ctx'), scatter_dimension=0, tiled=True)  113 us
    reduce_scatter x1, waiting for transfers between devices, on_device(): lax.psum_scatter(grad_down, ('shard', 'ctx'), scatter_dimension=1, tiled=...  79.1 us
    unnamed x14, waiting for transfers between devices  63.5 us
    psum x1, blocking collectives, on_device(): lax.psum((bias_terms, vector_terms), ('shard', 'ctx'))  62.4 us
    reduce_scatter x1, waiting for transfers between devices, on_device(): lax.psum_scatter(result_state[1].astype(jnp.bfloat16), 'ctx', scatter_dim...  59.9 us
    reduce_scatter x1, waiting for transfers between devices, on_device(): lax.psum_scatter(grad_out, ('shard', 'ctx'), scatter_dimension=1, tiled=T...  59.6 us
    all_gather x1, waiting for transfers between devices, on_device(): lax.all_gather(w_gu.astype(jnp.bfloat16), ('shard', 'ctx'), axis=0, tiled...  53.9 us
    psum x1, waiting for transfers between devices, on_device(): grad_hidden = grad_second + lax.psum(hidden_part, 'tp')  49.7 us
  transfers between devices with their start and end apart: 13, of which 12 were waited for; matrix products, arithmetic and copies ran while one was open for 5% of the time, Pallas kernels for 0%

commit v1 on v0

--- a/solution.py
+++ b/solution.py
@@ -134,7 +134,7 @@
     activated, unit_pull = jax.vjp(gated_unit, gated[:, :, 0], gated[:, :, 1])
     act_low = activated.astype(jnp.bfloat16)
     ffn_part = jnp.einsum("stf,fn->stn", act_low, whole_down, preferred_element_type=jnp.float32)
-    ffn_branch = lax.psum(ffn_part, "tp") + vectors[5]
+    ffn_branch = jnp.sum(lax.all_gather(ffn_part, "tp"), axis=0) + vectors[5]
     normed, second_pull = jax.vjp(layer_norm, hidden + ffn_branch, vectors[2], vectors[3])
     output = (normed * live_rows).astype(jnp.bfloat16)
     upstream = cotangent.astype(jnp.float32) * live_rows

time: 1020 us -> 1020 us (level)
    psum x1 -> x0, waiting for transfers between devices: 48.5 us -> none  [on_device(): ffn_branch = lax.psum(ffn_part, 'tp') + vectors[5]]
    all_gather x0 -> x1, waiting for transfers between devices: none -> 41.8 us  [on_device(): ffn_branch = jnp.sum(lax.all_gather(ffn_part, 'tp'), axis=0) + vectors[5]]
where the time goes in v1:
time: 1020 us
  waiting for transfers between devices  664 us (65%)
  blocking collectives  109 us (11%)
  local copies, waits for them, and re-layouts  94.2 us (9%)
  matrix products  63.9 us (6%)
  other arithmetic  53.3 us (5%)
  loops' own time  16.9 us (2%)
  between operations  15.4 us (2%)
    reduce_scatter x1, waiting for transfers between devices, on_device(): lax.psum_scatter(grad_gu, ('shard', 'ctx'), scatter_dimension=0, tiled=True)  113 us
    reduce_scatter x1, waiting for transfers between devices, on_device(): lax.psum_scatter(grad_down, ('shard', 'ctx'), scatter_dimension=1, tiled=...  79.1 us
    unnamed x14, waiting for transfers between devices  63.7 us
    psum x1, blocking collectives, on_device(): lax.psum((bias_terms, vector_terms), ('shard', 'ctx'))  62.3 us
    reduce_scatter x1, waiting for transfers between devices, on_device(): lax.psum_scatter(result_state[1].astype(jnp.bfloat16), 'ctx', scatter_dim...  59.9 us
    reduce_scatter x1, waiting for transfers between devices, on_device(): lax.psum_scatter(grad_out, ('shard', 'ctx'), scatter_dimension=1, tiled=T...  59.6 us
    all_gather x1, waiting for transfers between devices, on_device(): lax.all_gather(w_gu.astype(jnp.bfloat16), ('shard', 'ctx'), axis=0, tiled...  53.9 us
    psum x1, waiting for transfers between devices, on_device(): grad_hidden = grad_second + lax.psum(hidden_part, 'tp')  49.8 us
  transfers between devices with their start and end apart: 13, of which 12 were waited for; matrix products, arithmetic and copies ran while one was open for 5% of the time, Pallas kernels for 0%

profile of v1, /device:TPU:0, one launch (start us, length us, event | category | flops | bytes accessed | tf_op | source)
XLA Modules:
  0.0 1018.4 jit_solution(14344421614752813949)
XLA Ops:
  9.7 44.3 %all-gather.7.cloned.1.call-done = bf16[768,3,384]{2,0,1:T(8,128)(2,1)} async-done(((bf16[48,3,384]{2,0,1:T(8,128)(2,1)}), bf16[768,3,384]{2,0,1:T(8,128)(2,1)}) %all-gather.7.cloned.1.call-update) | async-done | bytes 1769488 | tf_op jit(solution)/shard_map/all_gather | solution.py:89
  60.1 47.1 %all_gather.24 = bf16[384,768]{0,1:T(8,128)(2,1)S(1)} all-gather(bf16[384,48]{0,1:T(8,128)(2,1)S(1)} %convert_element_type.137), channel_id=1, replica_groups=mesh['shard'=4,'ctx'=4,'tp'=2] {'shard','ctx'}, dimensions={1}, use_global_device_ids=true | all-gather | bytes 626688 | tf_op jit(solution)/shard_map/all_gather | solution.py:90
  107.6 22.3 %all-gather.9.cloned.1.call-done = bf16[2,1024,2,384]{3,1,2,0:T(8,128)(2,1)} async-done(((bf16[2,256,2,384]{3,1,2,0:T(8,128)(2,1)}), bf16[2,1024,2,384]{3,1,2,0:T(8,128)(2,1)}) %all-gather.9.cloned.1.call-update) | async-done | bytes 3145744 | tf_op jit(solution)/shard_map/all_gather | solution.py:104
  129.9 4.7 copy.62
  134.6 29.5 %while.26 = (s32[]{:T(128)}, f32[2,6,256,64]{2,3,1,0:T(8,128)S(1)}, f32[2,6,256]{2,1,0:T(8,128)S(1)}, s32[8,128]{1,0:T(8,128)}, s32[2]{0:T(128)}, /*index=5*/bf1...) while((s32[]{:T(128)}, f32[2,6,256,64]{2,3,1,0:T(8,128)S(1)}, ...), condition=%wide.region_2.3_spmd.clone, body=%wide.region_0.2_spmd.clone.sunk | while | flops 103321416 | bytes 7393984 | solution.py:121
  169.0 48.1 %all-reduce.7.cloned.1.call-done = f32[2,256,768]{2,1,0:T(8,128)} async-done(((f32[2,256,768]{2,1,0:T(8,128)}), f32[2,256,768]{2,1,0:T(8,128)}) %all-reduce.7.cloned.1.call-update) | async-done | bytes 1572880 | tf_op jit(solution)/shard_map/psum | solution.py:130
  219.1 53.9 %all-gather.11.cloned.1.call-done = bf16[768,2,1536]{2,0,1:T(8,128)(2,1)} async-done(((bf16[48,2,1536]{2,0,1:T(8,128)(2,1)}), bf16[768,2,1536]{2,0,1:T(8,128)(2,1)}) %all-gather.11.cloned.1.call-update) | async-done | bytes 4718608 | tf_op jit(solution)/shard_map/all_gather | solution.py:91
  273.0 4.7 fusion.23
  280.4 7.7 multiply_convert_fusion.1
  288.1 28.5 %all-gather.13.cloned.1.call-done = bf16[1536,768]{0,1:T(8,128)(2,1)} async-done(((bf16[1536,48]{0,1:T(8,128)(2,1)}), bf16[1536,768]{0,1:T(8,128)(2,1)}) %all-gather.13.cloned.1.call-update) | async-done | bytes 2359312 | tf_op jit(solution)/shard_map/all_gather | solution.py:92
  316.6 4.2 fusion.48
  322.8 41.8 %all-gather.15.cloned.1.call-done = f32[4,256,768]{2,1,0:T(8,128)} async-done(((f32[2,256,768]{2,1,0:T(8,128)}), f32[4,256,768]{2,1,0:T(8,128)}) %all-gather.15.cloned.1.call-update) | async-done | bytes 3145744 | tf_op jit(solution)/shard_map/all_gather | solution.py:137
  380.1 3.8 fusion.60
  385.8 49.8 %all-reduce.9.cloned.1.call-done = f32[2,256,768]{2,1,0:T(8,128)} async-done(((f32[2,256,768]{2,1,0:T(8,128)}), f32[2,256,768]{2,1,0:T(8,128)}) %all-reduce.9.cloned.1.call-update) | async-done | bytes 1572880 | tf_op jit(solution)/shard_map/psum | solution.py:154
  435.6 4.5 multiply_reduce_fusion.1
  446.1 88.9 %while.27 = (s32[]{:T(128)}, f32[2,256,6,64]{1,3,2,0:T(8,128)S(1)}, bf16[2,1024,2,384]{3,1,2,0:T(8,128)(2,1)}, bf16[8,2,128,2,384]{2,4,1,3,0:T(8,128)(2,1)}, s32...) while((s32[]{:T(128)}, f32[2,256,6,64]{1,3,2,0:T(8,128)S(1)}, ...), condition=%wide.region_16.17_spmd.clone, body=%wide.region_15.16_spmd.clone.sunk | while | flops 255492928 | bytes 16990992 | solution.py:213
  464.5 3.6 dynamic_update_slice.5
  475.7 3.6 dynamic_update_slice.5
  486.9 3.6 dynamic_update_slice.5
  498.1 3.6 dynamic_update_slice.5
  509.3 3.6 dynamic_update_slice.5
  520.5 3.6 dynamic_update_slice.5
  535.6 59.9 %reduce-scatter.5.cloned.1.call-done = bf16[2,256,2,384]{3,1,2,0:T(8,128)(2,1)} async-done(((bf16[2,1024,2,384]{3,1,2,0:T(8,128)(2,1)}), bf16[2,256,2,384]{3,1,2,0:T(8,128)(2,1)}) %reduce-scatter.5.cloned.1.call-update) | async-done | bytes 786448 | tf_op jit(solution)/shard_map/reduce_scatter | solution.py:214
  595.5 4.0 bitcast_convert_fusion
  602.5 6.3 copy.71
  610.7 7.9 convolution_bitcast_fusion.1
  621.6 3.6 convolution_bitcast_fusion.2
  627.5 62.3 %all-reduce.1 = (f32[2,384]{1,0:T(2,128)}, f32[6,768]{1,0:T(8,128)}) all-reduce(f32[2,384]{1,0:T(2,128)S(1)} %pad_maximum_fusion.10, f32[6,768]{1,0:T(8,128)S(1)} %stack.63), channel_id=1, replica_groups=mesh['shard'=4,'ctx'=4,'tp'=2] {'shard','ctx'}, use_global_device_ids=true, to_apply=%region_22.23 | all-reduce | flops 5376 | bytes 43008 | tf_op jit(solution)/shard_map/psum | solution.py:241
  692.4 63.5 %all-reduce.13.cloned.1.call-done = f32[768,3,384]{2,1,0:T(4,128)} async-done(((f32[768,3,384]{2,1,0:T(4,128)}), f32[768,3,384]{2,1,0:T(4,128)}) %all-reduce.13.cloned.1.call-update) | async-done | bytes 3538960
  757.5 113.3 %reduce-scatter.9.cloned.1.call-done = f32[48,2,1536]{2,0,1:T(8,128)} async-done(((f32[768,2,1536]{2,0,1:T(8,128)}), f32[48,2,1536]{2,0,1:T(8,128)}) %reduce-scatter.9.cloned.1.call-update) | async-done | bytes 589840 | tf_op jit(solution)/shard_map/reduce_scatter | solution.py:235
  873.2 59.6 %reduce-scatter.7.cloned.1.call-done = f32[384,48]{0,1:T(8,128)} async-done(((f32[384,768]{0,1:T(8,128)}), f32[384,48]{0,1:T(8,128)}) %reduce-scatter.7.cloned.1.call-update) | async-done | bytes 73744 | tf_op jit(solution)/shard_map/reduce_scatter | solution.py:234
  932.8 79.1 %reduce-scatter.11.cloned.1.call-done = f32[1536,48]{0,1:T(8,128)} async-done(((f32[1536,768]{0,1:T(8,128)}), f32[1536,48]{0,1:T(8,128)}) %reduce-scatter.11.cloned.1.call-update) | async-done | bytes 294928 | tf_op jit(solution)/shard_map/reduce_scatter | solution.py:236
  (458 shorter events, 139.7 us)
Async XLA Ops:
  7.2 46.8 %all-gather.7.cloned.1.call-start = ((), (), s32[]{:S(2)}) async-start(), calls=%async_computation.4 | async-start | bytes 1880064 | tf_op jit(solution)/shard_map/all_gather | solution.py:89
  8.8 121.1 %all-gather.9.cloned.1.call-start = ((), (), s32[]{:S(2)}) async-start(), calls=%async_computation.5 | async-start | bytes 3932160 | tf_op jit(solution)/shard_map/all_gather | solution.py:104
  58.1 159.0 %all-reduce.7.cloned.1.call-start = ((), (), s32[]{:S(2)}) async-start(), calls=%async_computation.6 | async-start | bytes 3145728 | tf_op jit(solution)/shard_map/psum | solution.py:130
  58.2 49.3 %copy-start.60 = (s32[256]{0:T(256)}, s32[256]{0:T(256)S(1)}, u32[]{:S(2)}) copy-start(s32[256]{0:T(256)S(1)} %multiply_add_fusion.6) | copy-start | bytes 3076
  107.2 57.0 %copy-start.11 = (bf16[384,768]{0,1:T(8,128)(2,1)}, bf16[384,768]{0,1:T(8,128)(2,1)S(1)}, u32[]{:S(2)}) copy-start(bf16[384,768]{0,1:T(8,128)(2,1)S(1)} %all_gather.24) | copy-start | bytes 1769476
  134.6 29.6 %copy-start.42 = (f32[2,256]{1,0:T(2,128)S(1)}, f32[2,256]{1,0:T(2,128)}, u32[]{:S(2)}) copy-start(f32[2,256]{1,0:T(2,128)} %broadcast_subtract_fusion) | copy-start | bytes 6148
  166.6 50.5 %copy-start.18 = (bf16[2,256,768]{2,1,0:T(8,128)(2,1)S(1)}, bf16[2,256,768]{2,1,0:T(8,128)(2,1)}, u32[]{:S(2)}) copy-start(bf16[2,256,768]{2,1,0:T(8,128)(2,1)} %param.13) | copy-start | bytes 2359300
  166.6 106.4 %all-gather.11.cloned.1.call-start = ((), (), s32[]{:S(2)}) async-start(), calls=%async_computation.7 | async-start | bytes 5013504 | tf_op jit(solution)/shard_map/all_gather | solution.py:91
  167.5 149.1 %all-gather.13.cloned.1.call-start = ((), (), s32[]{:S(2)}) async-start(), calls=%async_computation.8 | async-start | bytes 2506752 | tf_op jit(solution)/shard_map/all_gather | solution.py:92
  168.3 196.4 %all-gather.15.cloned.1.call-start = ((), (), s32[]{:S(2)}) async-start(), calls=%async_computation.15 | async-start | bytes 4718592 | tf_op jit(solution)/shard_map/all_gather | solution.py:137
  169.0 104.0 %copy-start.30 = (f32[768]{0:T(1024)}, f32[768]{0:T(1024)S(1)}, u32[]{:S(2)}) copy-start(f32[768]{0:T(1024)S(1)} %get-tuple-element.239) | copy-start | bytes 9220
  169.0 104.0 %copy-start.57 = (f32[768]{0:T(1024)}, f32[768]{0:T(1024)S(1)}, u32[]{:S(2)}) copy-start(f32[768]{0:T(1024)S(1)} %get-tuple-element.238) | copy-start | bytes 9220
  218.7 221.4 %copy-start = (f32[2,256,768]{2,1,0:T(8,128)}, f32[2,256,768]{2,1,0:T(8,128)S(1)}, u32[]{:S(2)}) copy-start(f32[2,256,768]{2,1,0:T(8,128)S(1)} %get-tuple-element.302) | copy-start | bytes 4718596
  218.7 54.3 %copy-start.34 = (f32[2,256]{1,0:T(2,128)}, f32[2,256]{1,0:T(2,128)S(1)}, u32[]{:S(2)}) copy-start(f32[2,256]{1,0:T(2,128)S(1)} %broadcast_multiply_fusion.3) | copy-start | bytes 6148
  219.1 53.9 %copy-start.48 = (f32[2,256]{1,0:T(2,128)}, f32[2,256]{1,0:T(2,128)S(1)}, u32[]{:S(2)}) copy-start(f32[2,256]{1,0:T(2,128)S(1)} %multiply_reduce_fusion.5) | copy-start | bytes 6148
  219.1 53.9 %copy-start.39 = (f32[2,256]{1,0:T(2,128)}, f32[2,256]{1,0:T(2,128)S(1)}, u32[]{:S(2)}) copy-start(f32[2,256]{1,0:T(2,128)S(1)} %fusion.83) | copy-start | bytes 6148
  288.1 32.8 %copy-start.16 = (bf16[2,256,1536]{2,1,0:T(8,128)(2,1)}, bf16[2,256,1536]{2,1,0:T(8,128)(2,1)S(1)}, u32[]{:S(2)}) copy-start(bf16[2,256,1536]{2,1,0:T(8,128)(2,1)S(1)} %get-tuple-element.299) | copy-start | bytes 4718596
  320.9 114.7 %all-reduce.9.cloned.1.call-start = ((), (), s32[]{:S(2)}) async-start(), calls=%async_computation.9 | async-start | bytes 3145728 | tf_op jit(solution)/shard_map/psum | solution.py:154
  368.1 7.0 slice-start
  370.2 4.8 slice-start.1
  373.8 6.3 slice-start.2
  383.9 211.6 %reduce-scatter.5.cloned.1.call-start = ((), (), s32[]{:S(2)}) async-start(), calls=%async_computation.10 | async-start | bytes 3932160 | tf_op jit(solution)/shard_map/reduce_scatter | solution.py:214
  435.6 4.5 copy-start.35
  435.6 4.5 copy-start.40
  535.0 154.9 %all-reduce.11.cloned.1.call-start = ((), (), s32[]{:S(2)}) async-start(), calls=%async_computation.11 | async-start | bytes 1572864 | tf_op jit(solution)/shard_map/psum | solution.py:231
  535.6 64.0 %copy-start.19 = (bf16[2,256,768]{2,1,0:T(8,128)(2,1)S(1)}, bf16[2,256,768]{2,1,0:T(8,128)(2,1)}, u32[]{:S(2)}) copy-start(bf16[2,256,768]{2,1,0:T(8,128)(2,1)} %param.13) | copy-start | bytes 2359300
  599.5 156.3 %all-reduce.13.cloned.1.call-start = ((), (), s32[]{:S(2)}) async-start(), calls=%async_computation.16 | async-start | bytes 9437184
  608.8 262.1 %reduce-scatter.9.cloned.1.call-start = ((), (), s32[]{:S(2)}) async-start(), calls=%async_computation.13 | async-start | bytes 10027008 | tf_op jit(solution)/shard_map/reduce_scatter | solution.py:235
  618.6 314.1 %reduce-scatter.7.cloned.1.call-start = ((), (), s32[]{:S(2)}) async-start(), calls=%async_computation.12 | async-start | bytes 1253376 | tf_op jit(solution)/shard_map/reduce_scatter | solution.py:234
  621.5 390.3 %reduce-scatter.11.cloned.1.call-start = ((), (), s32[]{:S(2)}) async-start(), calls=%async_computation.14 | async-start | bytes 5013504 | tf_op jit(solution)/shard_map/reduce_scatter | solution.py:236
  625.3 64.6 %copy-start.6 = (f32[2,256,768]{2,1,0:T(8,128)S(1)}, f32[2,256,768]{2,1,0:T(8,128)}, u32[]{:S(2)}) copy-start(f32[2,256,768]{2,1,0:T(8,128)} %copy-done.5) | copy-start | bytes 4718596
  625.3 64.6 %copy-start.47 = (f32[2,256]{1,0:T(2,128)S(1)}, f32[2,256]{1,0:T(2,128)}, u32[]{:S(2)}) copy-start(f32[2,256]{1,0:T(2,128)} %copy-done.46) | copy-start | bytes 6148
  (53 other events, 104.4 us)
Sparse Core Ops, SparseCore 0:
  10.8 43.1 all-gather.6
  58.2 71.6 all-gather.8
  166.7 50.2 all-reduce.6
  219.8 53.1 all-gather.10
  275.7 40.8 all-gather.12
  321.0 43.6 all-gather.14
  384.1 51.5 all-reduce.8
  535.1 60.3 reduce-scatter.4
  599.7 34.2 all-reduce.10
  637.5 118.3 all-reduce.12
  759.9 110.8 reduce-scatter.8
  874.9 57.8 reduce-scatter.6
  937.2 74.5 reduce-scatter.10
